TPU v7x, 32 devices: a whole 2x2x4 slice. The times are simulated.
32 devices in a mesh: img: 8 (over z, core), pix: 4 (over y, x).
Axes of the slice: x: 2, y: 2, z: 4, core: 2. Of those that a mesh axis runs over, the one named last changes fastest.
Arguments:
- images: bfloat16 [25600, 16384], P('img', 'pix'), may hold values from -6 to 6
- classes: int32 [25600], P('img'), may hold values from 0 to 63
- ctf_table: bfloat16 [64, 16384], P(None, 'pix'), may hold values from -1 to 1, as said below
- weights: float32 [25600], P('img'), may hold values from 0.1 to 1
- probes: float32 [16384, 256], P('pix'), may hold values from -6 to 6
Outputs:
- basis: float32 [16384, 256], P('pix')
- factor: float32 [256, 256], replicated
Inputs may be any that keep to these rules, and one draw needn't show every extreme that they name: `ctf_table`: a smooth envelope over the pixel index times an independent magnitude and sign for each entry.
All inputs are finite; a program needn't handle non-finite values.
Results may differ from a plain program's by a relative error of at most 0.012.
Values may be sent and summed in bfloat16 or wider, within the bound.
No kernel may reach another device: no remote copies, remote signals or barrier semaphores. Data moves between devices by JAX's collectives and lax.ppermute only.
A program may use at most 128 MiB of HBM per device.

v0:
```python
import jax
import jax.numpy as jnp
from jax import lax
from jax.sharding import PartitionSpec as P

ITERS = 2


def per_device(images, classes, ctf_table, weights, probes):
    onehot = (classes[:, None] == jnp.arange(ctf_table.shape[0])[None, :]).astype(jnp.bfloat16)
    filters = jnp.dot(onehot, ctf_table, preferred_element_type=jnp.float32)
    filtered = (images.astype(jnp.float32) * filters).astype(jnp.bfloat16)
    current = probes
    factor = jnp.zeros((probes.shape[1], probes.shape[1]), jnp.float32)
    for sweep in range(ITERS):
        probe_half = current.astype(jnp.bfloat16)
        share_rows = filtered.shape[0] // lax.axis_size("pix")
        shares = lax.psum_scatter(
            jnp.dot(filtered, probe_half, preferred_element_type=jnp.float32),
            "pix",
            scatter_dimension=0,
            tiled=True,
        )
        weight_share = lax.dynamic_slice_in_dim(
            weights, lax.axis_index("pix") * share_rows, share_rows, 0
        )
        scaled_share = (weight_share[:, None] * shares).astype(jnp.bfloat16)
        scaled = lax.all_gather(scaled_share, "pix", axis=0, tiled=True)
        partial_sum = lax.dot_general(
            filtered, scaled, (((0,), (0,)), ((), ())), preferred_element_type=jnp.float32
        )
        image_sum = lax.psum(partial_sum, "img")
        gram_matrix = lax.psum(
            jnp.dot(image_sum.T, image_sum, precision=lax.Precision.HIGHEST), "pix"
        )
        factor = jnp.linalg.cholesky(gram_matrix)
        current = jax.scipy.linalg.solve_triangular(factor, image_sum.T, lower=True).T
    return (current, factor)


def solution(mesh):
    in_specs = (P("img", "pix"), P("img"), P(None, "pix"), P("img"), P("pix", None))
    out_specs = (P("pix", None), P())
    return jax.shard_map(
        per_device, mesh=mesh, in_specs=in_specs, out_specs=out_specs, check_vma=False
    )
```

profile of v0, /device:TPU:0, one launch (start us, length us, event | category | flops | bytes accessed | tf_op | source)
XLA Modules:
  0.0 707.9 jit_solution(17062650772016324928)
XLA Ops:
  7.2 1.0 copy-done
  8.2 21.5 %multiply_convert_fusion = bf16[3200,4096]{1,0:T(8,128)(2,1)} fusion(bf16[3200,4096]{1,0:T(8,128)(2,1)} %param.8, bf16[64,4096]{1,0:T(8,128)(2,1)S(1)} %copy-done, s32[3200]{0:T(1024)} %param.9), kind=kOutput, calls=%fused_computation.4 | convolution fusion | flops 1717248000 | bytes 52965888 | tf_op jit(solution)/shard_map/dot_general | solution.py:11
  29.7 14.4 %fusion.5 = f32[3200,256]{1,0:T(8,128)} fusion(bf16[3200,4096]{1,0:T(8,128)(2,1)} %multiply_convert_fusion, f32[4096,256]{1,0:T(8,128)} %param.12), kind=kOutput, calls=%fused_computation.14 | convolution fusion | flops 6711934976 | bytes 33685504 | tf_op jit(solution)/shard_map/dot_general | solution.py:19
  44.2 0.8 dynamic_slice.4
  45.0 47.0 %reduce-scatter.3.cloned.1.call-done = f32[800,256]{1,0:T(8,128)} async-done(((f32[3200,256]{1,0:T(8,128)}), f32[800,256]{1,0:T(8,128)}) %reduce-scatter.3.cloned.1.call-update) | async-done | bytes 819216 | tf_op jit(solution)/shard_map/reduce_scatter | solution.py:18
  92.0 2.1 multiply_convert_fusion.2
  94.2 31.7 %all-gather.3.cloned.1.call-done = bf16[3200,256]{1,0:T(8,128)(2,1)} async-done(((bf16[800,256]{1,0:T(8,128)(2,1)}), bf16[3200,256]{1,0:T(8,128)(2,1)}) %all-gather.3.cloned.1.call-update) | async-done | bytes 1638416 | tf_op jit(solution)/shard_map/all_gather | solution.py:28
  125.9 14.4 %fusion.30 = f32[4096,256]{1,0:T(8,128)} fusion(bf16[3200,4096]{1,0:T(8,128)(2,1)} %multiply_convert_fusion, bf16[3200,256]{1,0:T(8,128)(2,1)} %all-gather.3.cloned.1.call-done), kind=kOutput, calls=%fused_computation.66 | convolution fusion | flops 6710886400 | bytes 32047104 | tf_op jit(solution)/shard_map/dot_general | solution.py:29
  140.8 96.1 %all-reduce.6.cloned.1.call-done = f32[4096,256]{1,0:T(8,128)} async-done(((f32[4096,256]{1,0:T(8,128)}), f32[4096,256]{1,0:T(8,128)}) %all-reduce.6.cloned.1.call-update) | async-done | bytes 4194320 | tf_op jit(solution)/shard_map/psum | solution.py:32
  236.9 10.9 %fusion.31 = f32[256,256]{0,1:T(8,128)} fusion(f32[4096,256]{1,0:T(8,128)} %all-reduce.6.cloned.1.call-done), kind=kOutput, calls=%fused_computation.67 | convolution fusion | flops 3221225472 | bytes 4456448 | tf_op jit(solution)/shard_map/dot_general | solution.py:34
  248.1 43.0 %all-reduce.8.cloned.1.call-done = f32[256,256]{0,1:T(8,128)} async-done(((f32[256,256]{0,1:T(8,128)}), f32[256,256]{0,1:T(8,128)}) %all-reduce.8.cloned.1.call-update) | async-done | bytes 262160 | tf_op jit(solution)/shard_map/psum | solution.py:33
  291.1 1.1 copy.8
  292.2 1.0 fusion.9
  293.2 11.7 %cholesky.130 = f32[128,128]{1,0:T(8,128)S(1)} custom-call(f32[128,128]{1,0:T(8,128)S(1)} %cholesky.194), custom_call_target="Cholesky" | custom-call | tf_op jit(solution)/shard_map/jit(cholesky)/cholesky | solution.py:36
  305.0 9.8 %custom-call.13 = f32[1,128,128]{1,2,0:T(8,128)S(1)} custom-call(f32[1,128,128]{2,1,0:T(8,128)S(1)} %get-tuple-element.51), custom_call_target="InvertDiagBlocksLowerTriangular" | custom-call | tf_op jit(solution)/shard_map/jit(cholesky)/cholesky | solution.py:36
  315.3 11.7 %cholesky.147 = f32[128,128]{1,0:T(8,128)S(1)} custom-call(f32[128,128]{1,0:T(8,128)S(1)} %convolution_subtract_fusion.3), custom_call_target="Cholesky" | custom-call | tf_op jit(solution)/shard_map/jit(cholesky)/cholesky | solution.py:36
  327.0 0.7 compare_reduce_fusion.2
  329.1 4.2 while.4
  329.9 1.4 bitcast_dynamic-update-slice_fusion.4
  331.9 1.4 bitcast_dynamic-update-slice_fusion.4
  333.3 19.7 %custom-call.14 = f32[2,128,128]{1,2,0:T(8,128)S(1)} custom-call(f32[2,128,128]{2,1,0:T(8,128)S(1)} %get-tuple-element.18), custom_call_target="InvertDiagBlocksLowerTriangular" | custom-call | tf_op jit(solution)/shard_map/jit(_solve_triangular)/triangular_solve | solution.py:37
  353.0 3.7 fusion.3
  356.7 3.6 convolution_subtract_fusion.1
  360.3 1.9 fusion.17
  362.2 14.2 %fusion = f32[3200,256]{1,0:T(8,128)} fusion(bf16[3200,4096]{1,0:T(8,128)(2,1)} %multiply_convert_fusion, bf16[128,4096]{1,0:T(8,128)(2,1)S(1)} %fusion.17, f32[128,4096]{1,0:T(8,128)S(1)} %fusion.3), kind=kOutput, calls=%fused_computation.9 | convolution fusion | flops 6715080704 | bytes 32636928 | tf_op jit(solution)/shard_map/dot_general | solution.py:19
  376.5 45.1 %reduce-scatter.5.cloned.1.call-done = f32[800,256]{1,0:T(8,128)} async-done(((f32[3200,256]{1,0:T(8,128)}), f32[800,256]{1,0:T(8,128)}) %reduce-scatter.5.cloned.1.call-update) | async-done | bytes 819216 | tf_op jit(solution)/shard_map/reduce_scatter | solution.py:18
  421.6 2.1 multiply_convert_fusion.1
  423.7 31.5 %all-gather.5.cloned.1.call-done = bf16[3200,256]{1,0:T(8,128)(2,1)} async-done(((bf16[800,256]{1,0:T(8,128)(2,1)}), bf16[3200,256]{1,0:T(8,128)(2,1)}) %all-gather.5.cloned.1.call-update) | async-done | bytes 1638416 | tf_op jit(solution)/shard_map/all_gather | solution.py:28
  455.3 14.4 %fusion.32 = f32[4096,256]{1,0:T(8,128)} fusion(bf16[3200,4096]{1,0:T(8,128)(2,1)} %multiply_convert_fusion, bf16[3200,256]{1,0:T(8,128)(2,1)} %all-gather.5.cloned.1.call-done), kind=kOutput, calls=%fused_computation.68 | convolution fusion | flops 6710886400 | bytes 32047104 | tf_op jit(solution)/shard_map/dot_general | solution.py:29
  469.9 96.4 %all-reduce.10.cloned.1.call-done = f32[4096,256]{1,0:T(8,128)} async-done(((f32[4096,256]{1,0:T(8,128)}), f32[4096,256]{1,0:T(8,128)}) %all-reduce.10.cloned.1.call-update) | async-done | bytes 4194320 | tf_op jit(solution)/shard_map/psum | solution.py:32
  566.3 10.9 %fusion.33 = f32[256,256]{0,1:T(8,128)} fusion(f32[4096,256]{1,0:T(8,128)} %all-reduce.10.cloned.1.call-done), kind=kOutput, calls=%fused_computation.69 | convolution fusion | flops 3221225472 | bytes 4456448 | tf_op jit(solution)/shard_map/dot_general | solution.py:34
  577.3 43.2 %all-reduce.12.cloned.1.call-done = f32[256,256]{0,1:T(8,128)} async-done(((f32[256,256]{0,1:T(8,128)}), f32[256,256]{0,1:T(8,128)}) %all-reduce.12.cloned.1.call-update) | async-done | bytes 262160 | tf_op jit(solution)/shard_map/psum | solution.py:33
  620.5 1.1 copy.10
  621.6 1.0 fusion.8
  622.6 11.7 %cholesky.164 = f32[128,128]{1,0:T(8,128)S(1)} custom-call(f32[128,128]{1,0:T(8,128)S(1)} %cholesky.197), custom_call_target="Cholesky" | custom-call | tf_op jit(solution)/shard_map/jit(cholesky)/cholesky | solution.py:36
  634.4 10.0 %custom-call.15 = f32[1,128,128]{1,2,0:T(8,128)S(1)} custom-call(f32[1,128,128]{2,1,0:T(8,128)S(1)} %get-tuple-element.47), custom_call_target="InvertDiagBlocksLowerTriangular" | custom-call | tf_op jit(solution)/shard_map/jit(cholesky)/cholesky | solution.py:36
  644.9 11.7 %cholesky.181 = f32[128,128]{1,0:T(8,128)S(1)} custom-call(f32[128,128]{1,0:T(8,128)S(1)} %convolution_subtract_fusion.2), custom_call_target="Cholesky" | custom-call | tf_op jit(solution)/shard_map/jit(cholesky)/cholesky | solution.py:36
  656.6 0.6 compare_reduce_fusion
  659.2 0.7 fusion.11
  659.9 3.9 while.5
  660.5 1.4 bitcast_dynamic-update-slice_fusion.5
  662.5 1.4 bitcast_dynamic-update-slice_fusion.5
  663.9 19.7 %custom-call.16 = f32[2,128,128]{1,2,0:T(8,128)S(1)} custom-call(f32[2,128,128]{2,1,0:T(8,128)S(1)} %get-tuple-element.19), custom_call_target="InvertDiagBlocksLowerTriangular" | custom-call | tf_op jit(solution)/shard_map/jit(_solve_triangular)/triangular_solve | solution.py:37
  683.6 3.7 fusion.1
  687.3 3.4 convolution_subtract_fusion
  690.7 2.0 fusion.13
  692.7 2.4 maximum_bitcast_fusion
  695.1 5.6 copy.11
  (49 shorter events, 5.6 us)
Async XLA Ops:
  7.2 1.1 copy-start
  7.2 84.8 %reduce-scatter.3.cloned.1.call-start = ((), (), s32[]{:S(2)}) async-start(), calls=%async_computation.2 | async-start | bytes 4096000 | tf_op jit(solution)/shard_map/reduce_scatter | solution.py:18
  44.1 81.7 %all-gather.3.cloned.1.call-start = ((), (), s32[]{:S(2)}) async-start(), calls=%async_computation.3 | async-start | bytes 2048000 | tf_op jit(solution)/shard_map/all_gather | solution.py:28
  94.1 142.8 %all-reduce.6.cloned.1.call-start = ((), (), s32[]{:S(2)}) async-start(), calls=%async_computation.4 | async-start | bytes 8388608 | tf_op jit(solution)/shard_map/psum | solution.py:32
  140.3 150.8 %all-reduce.8.cloned.1.call-start = ((), (), s32[]{:S(2)}) async-start(), calls=%async_computation.5 | async-start | bytes 524288 | tf_op jit(solution)/shard_map/psum | solution.py:33
  247.9 173.7 %reduce-scatter.5.cloned.1.call-start = ((), (), s32[]{:S(2)}) async-start(), calls=%async_computation.6 | async-start | bytes 4096000 | tf_op jit(solution)/shard_map/reduce_scatter | solution.py:18
  353.0 3.7 copy-start.2
  376.4 78.8 %all-gather.5.cloned.1.call-start = ((), (), s32[]{:S(2)}) async-start(), calls=%async_computation.7 | async-start | bytes 2048000 | tf_op jit(solution)/shard_map/all_gather | solution.py:28
  423.7 142.6 %all-reduce.10.cloned.1.call-start = ((), (), s32[]{:S(2)}) async-start(), calls=%async_computation.8 | async-start | bytes 8388608 | tf_op jit(solution)/shard_map/psum | solution.py:32
  469.7 150.8 %all-reduce.12.cloned.1.call-start = ((), (), s32[]{:S(2)}) async-start(), calls=%async_computation.9 | async-start | bytes 524288 | tf_op jit(solution)/shard_map/psum | solution.py:33
  683.6 3.7 copy-start.3
  692.7 8.0 %copy-start.1 = (bf16[64,4096]{1,0:T(8,128)(2,1)S(1)}, bf16[64,4096]{1,0:T(8,128)(2,1)}, u32[]{:S(2)}) copy-start(bf16[64,4096]{1,0:T(8,128)(2,1)} %param.10) | copy-start | bytes 1572868
Sparse Core Ops, SparseCore 0:
  44.3 47.7 reduce-scatter.2
  94.4 31.3 all-gather.2
  140.4 96.4 all-reduce.5
  248.0 43.0 all-reduce.7
  376.6 44.9 reduce-scatter.4
  423.9 31.3 all-gather.4
  469.8 96.4 all-reduce.9
  577.4 43.0 all-reduce.11
where the time goes:
time: 716 us; the launch traced here: 708 us
  waiting for transfers between devices  434 us (61%)
  matrix products  120 us (17%)
  other arithmetic  117 us (16%)
  local copies, waits for them, and re-layouts  17.5 us (2%)
  between operations  17.3 us (2%)
    psum x2, waiting for transfers between devices, per_device(): image_sum = lax.psum(partial_sum, 'img')  193 us
    reduce_scatter x2, waiting for transfers between devices, per_device(): lax.psum_scatter(jnp.dot(filtered, probe_half, preferred_element_type=jnp...  92.2 us
    psum x2, waiting for transfers between devices, per_device(): lax.psum(jnp.dot(image_sum.T, image_sum, precision=lax.Precision.HIGHEST)...  86.3 us
    another operation x13, other arithmetic, per_device(): factor = jnp.linalg.cholesky(gram_matrix)  68.7 us
    all_gather x2, waiting for transfers between devices, per_device(): scaled = lax.all_gather(scaled_share, 'pix', axis=0, tiled=True)  63.2 us
    another operation x5, other arithmetic, per_device(): jax.scipy.linalg.solve_triangular(factor, image_sum.T, lower=True)  40.1 us
    dot_general x2, matrix products, per_device(): lax.dot_general(filtered, scaled, (((0,), (0,)), ((), ())), preferred_ele...  28.8 us
    dot_general x2, matrix products, per_device(): jnp.dot(filtered, probe_half, preferred_element_type=jnp.float32)  28.6 us
  transfers between devices with their start and end apart: 8, of which 8 were waited for; matrix products, arithmetic and copies ran while one was open for 0% of the time, Pallas kernels for 0%

commit v1 on v0

--- a/solution.py
+++ b/solution.py
@@ -29,7 +29,7 @@
         partial_sum = lax.dot_general(
             filtered, scaled, (((0,), (0,)), ((), ())), preferred_element_type=jnp.float32
         )
-        image_sum = lax.psum(partial_sum, "img")
+        image_sum = jnp.sum(lax.all_gather(partial_sum, "img"), axis=0)
         gram_matrix = lax.psum(
             jnp.dot(image_sum.T, image_sum, precision=lax.Precision.HIGHEST), "pix"
         )

time: 716 us -> 1130 us (1.58)
  waiting for transfers between devices: 434 us -> 815 us
  other arithmetic: 117 us -> 147 us
    all_gather x0 -> x2, waiting for transfers between devices: none -> 577 us  [per_device(): image_sum = jnp.sum(lax.all_gather(partial_sum, 'img'), axis=0)]
    psum x2 -> x0, waiting for transfers between devices: 193 us -> none  [per_device(): image_sum = lax.psum(partial_sum, 'img')]
    reduce_sum x0 -> x2, other arithmetic: none -> 28.8 us  [per_device(): image_sum = jnp.sum(lax.all_gather(partial_sum, 'img'), axis=0)]
where the time goes in v1:
time: 1130 us; the launch traced here: 1120 us
  waiting for transfers between devices  815 us (72%)
  other arithmetic  147 us (13%)
  matrix products  120 us (11%)
  local copies, waits for them, and re-layouts  17.8 us (2%)
  between operations  17.5 us (2%)
    all_gather x2, waiting for transfers between devices, per_device(): image_sum = jnp.sum(lax.all_gather(partial_sum, 'img'), axis=0)  577 us
    reduce_scatter x2, waiting for transfers between devices, per_device(): lax.psum_scatter(jnp.dot(filtered, probe_half, preferred_element_type=jnp...  92.1 us
    psum x2, waiting for transfers between devices, per_device(): lax.psum(jnp.dot(image_sum.T, image_sum, precision=lax.Precision.HIGHEST)...  82.5 us
    another operation x13, other arithmetic, per_device(): factor = jnp.linalg.cholesky(gram_matrix)  68.9 us
    all_gather x2, waiting for transfers between devices, per_device(): scaled = lax.all_gather(scaled_share, 'pix', axis=0, tiled=True)  63.2 us
    another operation x5, other arithmetic, per_device(): jax.scipy.linalg.solve_triangular(factor, image_sum.T, lower=True)  40.4 us
    reduce_sum x2, other arithmetic, per_device(): image_sum = jnp.sum(lax.all_gather(partial_sum, 'img'), axis=0)  28.8 us
    dot_general x2, matrix products, per_device(): lax.dot_general(filtered, scaled, (((0,), (0,)), ((), ())), preferred_ele...  28.8 us
  transfers between devices with their start and end apart: 8, of which 8 were waited for; matrix products, arithmetic and copies ran while one was open for 0% of the time, Pallas kernels for 0%

profile of v1, /device:TPU:0, one launch (start us, length us, event | category | flops | bytes accessed | tf_op | source)
XLA Modules:
  0.0 1117.9 jit_solution(2997258464826088800)
XLA Ops:
  7.2 1.0 copy-done
  8.2 21.4 %multiply_convert_fusion = bf16[3200,4096]{1,0:T(8,128)(2,1)} fusion(bf16[3200,4096]{1,0:T(8,128)(2,1)} %param.8, bf16[64,4096]{1,0:T(8,128)(2,1)S(1)} %copy-done, s32[3200]{0:T(1024)} %param.9), kind=kOutput, calls=%fused_computation.4 | convolution fusion | flops 1717248000 | bytes 52965888 | tf_op jit(solution)/shard_map/dot_general | solution.py:11
  29.7 14.4 %fusion.5 = f32[3200,256]{1,0:T(8,128)} fusion(bf16[3200,4096]{1,0:T(8,128)(2,1)} %multiply_convert_fusion, f32[4096,256]{1,0:T(8,128)} %param.12), kind=kOutput, calls=%fused_computation.14 | convolution fusion | flops 6711934976 | bytes 33685504 | tf_op jit(solution)/shard_map/dot_general | solution.py:19
  44.2 0.8 dynamic_slice.4
  44.9 47.0 %reduce-scatter.3.cloned.1.call-done = f32[800,256]{1,0:T(8,128)} async-done(((f32[3200,256]{1,0:T(8,128)}), f32[800,256]{1,0:T(8,128)}) %reduce-scatter.3.cloned.1.call-update) | async-done | bytes 819216 | tf_op jit(solution)/shard_map/reduce_scatter | solution.py:18
  92.0 2.1 multiply_convert_fusion.2
  94.1 31.7 %all-gather.7.cloned.1.call-done = bf16[3200,256]{1,0:T(8,128)(2,1)} async-done(((bf16[800,256]{1,0:T(8,128)(2,1)}), bf16[3200,256]{1,0:T(8,128)(2,1)}) %all-gather.7.cloned.1.call-update) | async-done | bytes 1638416 | tf_op jit(solution)/shard_map/all_gather | solution.py:28
  125.8 14.4 %fusion.30 = f32[4096,256]{1,0:T(8,128)} fusion(bf16[3200,4096]{1,0:T(8,128)(2,1)} %multiply_convert_fusion, bf16[3200,256]{1,0:T(8,128)(2,1)} %all-gather.7.cloned.1.call-done), kind=kOutput, calls=%fused_computation.66 | convolution fusion | flops 6710886400 | bytes 32047104 | tf_op jit(solution)/shard_map/dot_general | solution.py:29
  140.8 288.2 %all-gather.11.cloned.1.call-done = f32[32768,256]{1,0:T(8,128)} async-done(((f32[4096,256]{1,0:T(8,128)}), f32[32768,256]{1,0:T(8,128)}) %all-gather.11.cloned.1.call-update) | async-done | bytes 33554448 | tf_op jit(solution)/shard_map/all_gather | solution.py:32
  429.0 14.3 %reduce_sum.18 = f32[4096,256]{1,0:T(8,128)} reduce(f32[8,4096,256]{2,1,0:T(8,128)} %bitcast.83, f32[]{:T(128)} %constant.69.clone.1), dimensions={0}, to_apply=%region_1.0 | reduce | flops 7340032 | bytes 37748740 | tf_op jit(solution)/shard_map/reduce_sum | solution.py:32
  443.3 10.9 fusion.31
  454.4 41.2 %all-reduce.4.cloned.1.call-done = f32[256,256]{0,1:T(8,128)} async-done(((f32[256,256]{0,1:T(8,128)}), f32[256,256]{0,1:T(8,128)}) %all-reduce.4.cloned.1.call-update) | async-done | bytes 262160 | tf_op jit(solution)/shard_map/psum | solution.py:33
  495.6 1.1 copy.8
  496.7 1.0 fusion.9
  497.7 11.7 %cholesky.130 = f32[128,128]{1,0:T(8,128)S(1)} custom-call(f32[128,128]{1,0:T(8,128)S(1)} %cholesky.194), custom_call_target="Cholesky" | custom-call | tf_op jit(solution)/shard_map/jit(cholesky)/cholesky | solution.py:36
  509.4 9.8 custom-call.13
  519.7 11.7 %cholesky.147 = f32[128,128]{1,0:T(8,128)S(1)} custom-call(f32[128,128]{1,0:T(8,128)S(1)} %convolution_subtract_fusion.3), custom_call_target="Cholesky" | custom-call | tf_op jit(solution)/shard_map/jit(cholesky)/cholesky | solution.py:36
  533.7 4.3 while.4
  534.5 1.4 bitcast_dynamic-update-slice_fusion.4
  536.6 1.4 bitcast_dynamic-update-slice_fusion.4
  538.0 19.7 %custom-call.14 = f32[2,128,128]{1,2,0:T(8,128)S(1)} custom-call(f32[2,128,128]{2,1,0:T(8,128)S(1)} %get-tuple-element.18), custom_call_target="InvertDiagBlocksLowerTriangular" | custom-call | tf_op jit(solution)/shard_map/jit(_solve_triangular)/triangular_solve | solution.py:37
  557.7 3.7 fusion.3
  561.4 3.6 convolution_subtract_fusion.1
  565.0 1.9 fusion.17
  566.9 14.2 %fusion = f32[3200,256]{1,0:T(8,128)} fusion(bf16[3200,4096]{1,0:T(8,128)(2,1)} %multiply_convert_fusion, bf16[128,4096]{1,0:T(8,128)(2,1)S(1)} %fusion.17, f32[128,4096]{1,0:T(8,128)S(1)} %fusion.3), kind=kOutput, calls=%fused_computation.9 | convolution fusion | flops 6715080704 | bytes 32636928 | tf_op jit(solution)/shard_map/dot_general | solution.py:19
  581.2 45.1 %reduce-scatter.5.cloned.1.call-done = f32[800,256]{1,0:T(8,128)} async-done(((f32[3200,256]{1,0:T(8,128)}), f32[800,256]{1,0:T(8,128)}) %reduce-scatter.5.cloned.1.call-update) | async-done | bytes 819216 | tf_op jit(solution)/shard_map/reduce_scatter | solution.py:18
  626.3 2.1 multiply_convert_fusion.1
  628.5 31.5 %all-gather.9.cloned.1.call-done = bf16[3200,256]{1,0:T(8,128)(2,1)} async-done(((bf16[800,256]{1,0:T(8,128)(2,1)}), bf16[3200,256]{1,0:T(8,128)(2,1)}) %all-gather.9.cloned.1.call-update) | async-done | bytes 1638416 | tf_op jit(solution)/shard_map/all_gather | solution.py:28
  660.0 14.4 %fusion.32 = f32[4096,256]{1,0:T(8,128)} fusion(bf16[3200,4096]{1,0:T(8,128)(2,1)} %multiply_convert_fusion, bf16[3200,256]{1,0:T(8,128)(2,1)} %all-gather.9.cloned.1.call-done), kind=kOutput, calls=%fused_computation.68 | convolution fusion | flops 6710886400 | bytes 32047104 | tf_op jit(solution)/shard_map/dot_general | solution.py:29
  674.5 288.7 %all-gather.13.cloned.1.call-done = f32[32768,256]{1,0:T(8,128)} async-done(((f32[4096,256]{1,0:T(8,128)}), f32[32768,256]{1,0:T(8,128)}) %all-gather.13.cloned.1.call-update) | async-done | bytes 33554448 | tf_op jit(solution)/shard_map/all_gather | solution.py:32
  963.2 14.5 %reduce_sum.19 = f32[4096,256]{1,0:T(8,128)} reduce(f32[8,4096,256]{2,1,0:T(8,128)} %bitcast.84, f32[]{:T(128)} %constant.69.clone.1), dimensions={0}, to_apply=%region_8.11 | reduce | flops 7340032 | bytes 37748740 | tf_op jit(solution)/shard_map/reduce_sum | solution.py:32
  977.7 10.9 fusion.33
  988.6 41.4 %all-reduce.6.cloned.1.call-done = f32[256,256]{0,1:T(8,128)} async-done(((f32[256,256]{0,1:T(8,128)}), f32[256,256]{0,1:T(8,128)}) %all-reduce.6.cloned.1.call-update) | async-done | bytes 262160 | tf_op jit(solution)/shard_map/psum | solution.py:33
  1030.0 1.1 copy.10
  1031.0 1.0 fusion.8
  1032.0 11.7 %cholesky.164 = f32[128,128]{1,0:T(8,128)S(1)} custom-call(f32[128,128]{1,0:T(8,128)S(1)} %cholesky.197), custom_call_target="Cholesky" | custom-call | tf_op jit(solution)/shard_map/jit(cholesky)/cholesky | solution.py:36
  1043.8 10.0 custom-call.15
  1054.3 11.7 %cholesky.181 = f32[128,128]{1,0:T(8,128)S(1)} custom-call(f32[128,128]{1,0:T(8,128)S(1)} %convolution_subtract_fusion.2), custom_call_target="Cholesky" | custom-call | tf_op jit(solution)/shard_map/jit(cholesky)/cholesky | solution.py:36
  1068.7 0.7 fusion.11
  1069.5 4.1 while.5
  1070.2 1.3 bitcast_dynamic-update-slice_fusion.5
  1072.2 1.3 bitcast_dynamic-update-slice_fusion.5
  1073.6 19.9 %custom-call.16 = f32[2,128,128]{1,2,0:T(8,128)S(1)} custom-call(f32[2,128,128]{2,1,0:T(8,128)S(1)} %get-tuple-element.19), custom_call_target="InvertDiagBlocksLowerTriangular" | custom-call | tf_op jit(solution)/shard_map/jit(_solve_triangular)/triangular_solve | solution.py:37
  1093.5 3.7 fusion.1
  1097.2 3.4 convolution_subtract_fusion
  1100.7 2.0 fusion.13
  1102.7 2.4 maximum_bitcast_fusion
  1105.1 5.6 copy.11
  (51 shorter events, 7.1 us)
Async XLA Ops:
  7.2 1.1 copy-start
  7.2 84.8 %reduce-scatter.3.cloned.1.call-start = ((), (), s32[]{:S(2)}) async-start(), calls=%async_computation.2 | async-start | bytes 4096000 | tf_op jit(solution)/shard_map/reduce_scatter | solution.py:18
  44.1 81.7 %all-gather.7.cloned.1.call-start = ((), (), s32[]{:S(2)}) async-start(), calls=%async_computation.3 | async-start | bytes 2048000 | tf_op jit(solution)/shard_map/all_gather | solution.py:28
  94.0 334.9 %all-gather.11.cloned.1.call-start = ((), (), s32[]{:S(2)}) async-start(), calls=%async_computation.8 | async-start | bytes 37748736 | tf_op jit(solution)/shard_map/all_gather | solution.py:32
  140.2 355.4 %all-reduce.4.cloned.1.call-start = ((), (), s32[]{:S(2)}) async-start(), calls=%async_computation.4 | async-start | bytes 524288 | tf_op jit(solution)/shard_map/psum | solution.py:33
  454.2 172.1 %reduce-scatter.5.cloned.1.call-start = ((), (), s32[]{:S(2)}) async-start(), calls=%async_computation.5 | async-start | bytes 4096000 | tf_op jit(solution)/shard_map/reduce_scatter | solution.py:18
  557.7 3.7 copy-start.2
  581.1 78.8 %all-gather.9.cloned.1.call-start = ((), (), s32[]{:S(2)}) async-start(), calls=%async_computation.6 | async-start | bytes 2048000 | tf_op jit(solution)/shard_map/all_gather | solution.py:28
  628.4 334.8 %all-gather.13.cloned.1.call-start = ((), (), s32[]{:S(2)}) async-start(), calls=%async_computation.9 | async-start | bytes 37748736 | tf_op jit(solution)/shard_map/all_gather | solution.py:32
  674.4 355.5 %all-reduce.6.cloned.1.call-start = ((), (), s32[]{:S(2)}) async-start(), calls=%async_computation.7 | async-start | bytes 524288 | tf_op jit(solution)/shard_map/psum | solution.py:33
  1093.5 3.7 copy-start.3
  1102.6 8.0 copy-start.1
Sparse Core Ops, SparseCore 0:
  44.2 47.6 reduce-scatter.2
  94.4 31.3 all-gather.6
  140.3 288.5 all-gather.10
  454.3 41.2 all-reduce.3
  581.3 44.9 reduce-scatter.4
  628.6 31.3 all-gather.8
  674.5 288.5 all-gather.12
  988.7 41.2 all-reduce.5
